TPU v7x, 128 devices: a whole 4x4x4 slice. The times are simulated.
128 devices in a mesh: blk: 64 (over z, y, x_hi, core), rows: 2 (over x_lo).
Axes of the slice: x: 4 (x_hi: 2, x_lo: 2; x = x_hi * 2 + x_lo), y: 4, z: 4, core: 2. Of those that a mesh axis runs over, the one named last changes fastest.
Arguments:
- panel: bfloat16 [4, 512, 393216], P(None, 'rows', 'blk'), may hold values from -0.009765625 to 0.009765625
- solved: bfloat16 [393216, 1024], P('blk'), may hold values from -6 to 6
- loads: float32 [4, 512, 1024], P(None, 'rows'), may hold values from -6 to 6
- window: bfloat16 [4, 512, 2048], P(None, 'rows'), may hold values from -0.25 to 0.25
- inverses: bfloat16 [4, 512, 512], P(None, 'rows'), as said below
Outputs:
- unknowns: bfloat16 [4, 512, 1024], P(None, 'rows')
Inputs may be any that keep to these rules, and one draw needn't show every extreme that they name: inverses[i] is lower triangular, the inverse of the factor's i-th diagonal block.
All inputs are finite; a program needn't handle non-finite values.
Results may differ from a plain program's by a relative error of at most 0.01.
Values may be sent and summed in bfloat16 or wider, within the bound.
A program may use at most 128 MiB of HBM per device.

v0:
```python
import jax
import jax.numpy as jnp
from jax import lax
from jax.sharding import PartitionSpec as P


def shards(panel, solved, loads, window, inverses):
    partial_value = jnp.einsum("ksc,cr->ksr", panel, solved, preferred_element_type=jnp.float32)
    totals = lax.psum(partial_value, "blk")
    remaining = loads - totals
    block_size = inverses.shape[2]
    step_count = loads.shape[0]
    full_blocks = []
    own_rows = []
    for current in range(step_count):
        residual = remaining[current]
        for earlier in range(current):
            coupling = window[current][:, earlier * block_size : (earlier + 1) * block_size]
            residual = residual - jnp.dot(
                coupling, full_blocks[earlier], preferred_element_type=jnp.float32
            )
        residual = residual.astype(jnp.bfloat16)
        inverse_now = inverses[current]
        solved_part = jnp.dot(
            inverse_now,
            lax.all_gather(residual, "rows", axis=0, tiled=True),
            preferred_element_type=jnp.float32,
        ).astype(jnp.bfloat16)
        own_rows.append(solved_part)
        if current + 1 < step_count:
            full_blocks.append(lax.all_gather(solved_part, "rows", axis=0, tiled=True))
    result = jnp.stack(own_rows)
    return result


def solution(mesh):
    placed = (
        P(None, "rows", "blk"),
        P("blk", None),
        P(None, "rows", None),
        P(None, "rows", None),
        P(None, "rows", None),
    )
    return jax.shard_map(
        shards, mesh=mesh, in_specs=placed, out_specs=P(None, "rows", None), check_vma=False
    )
```

profile of v0, /device:TPU:1, one launch (start us, length us, event | category | flops | bytes accessed | tf_op | source)
XLA Modules:
  0.0 892.1 jit_solution(10524054517992434693)
XLA Ops:
  6.5 0.0 all-reduce.2.cloned.1.call-start
  6.5 19.0 %fusion = f32[4,256,1024]{2,1,0:T(8,128)} fusion(bf16[4,256,6144]{2,1,0:T(8,128)(2,1)} %param.5, bf16[6144,1024]{1,0:T(8,128)(2,1)} %param.6), kind=kOutput, calls=%fused_computation | convolution fusion | flops 12884901888 | bytes 29360128 | tf_op jit(solution)/shard_map/ksc,cr->ksr/dot_general | solution.py:8
  25.6 0.0 all-reduce.2.cloned.1.call-update
  25.6 0.0 all-gather.21.cloned.1.call-start
  25.7 653.3 %all-reduce.2.cloned.1.call-done = f32[4,256,1024]{2,1,0:T(8,128)} async-done(((f32[4,256,1024]{2,1,0:T(8,128)}), f32[4,256,1024]{2,1,0:T(8,128)}) %all-reduce.2.cloned.1.call-update) | async-done | bytes 4194320 | tf_op jit(solution)/shard_map/psum | solution.py:9
  679.0 4.4 sub.21
  683.4 0.0 copy-start
  683.4 1.9 copy-done
  685.3 0.9 slice.123
  686.2 0.0 all-gather.21.cloned.1.call-update
  686.2 0.0 all-gather.9.cloned.1.call-start
  686.3 24.5 %all-gather.21.cloned.1.call-done = bf16[1,512,1024]{2,1,0:T(8,128)(2,1)} async-done(((bf16[1,256,1024]{2,1,0:T(8,128)(2,1)}), bf16[1,512,1024]{2,1,0:T(8,128)(2,1)}) %all-gather.21.cloned.1.call-update) | async-done | bytes 1048592 | tf_op jit(solution)/shard_map/all_gather | solution.py:26
  710.7 2.6 convolution_convert_fusion.3
  713.3 0.0 all-gather.9.cloned.1.call-update
  713.3 0.0 all-gather.11.cloned.1.call-start
  713.4 3.1 slice_bitcast_fusion.3
  716.5 21.7 %all-gather.9.cloned.1.call-done = bf16[512,1024]{0,1:T(8,128)(2,1)} async-done(((bf16[256,1024]{0,1:T(8,128)(2,1)}), bf16[512,1024]{0,1:T(8,128)(2,1)}) %all-gather.9.cloned.1.call-update) | async-done | bytes 1048592 | tf_op jit(solution)/shard_map/all_gather | solution.py:31
  738.2 0.0 copy-start.1
  738.2 2.9 fusion.10
  741.1 0.0 all-gather.11.cloned.1.call-update
  741.1 0.0 all-gather.13.cloned.1.call-start
  741.2 24.9 %all-gather.11.cloned.1.call-done = bf16[512,1024]{1,0:T(8,128)(2,1)} async-done(((bf16[256,1024]{1,0:T(8,128)(2,1)}), bf16[512,1024]{1,0:T(8,128)(2,1)}) %all-gather.11.cloned.1.call-update) | async-done | bytes 1048592 | tf_op jit(solution)/shard_map/all_gather | solution.py:26
  766.1 2.6 convolution_convert_fusion.2
  768.6 0.0 all-gather.13.cloned.1.call-update
  768.6 0.0 all-gather.15.cloned.1.call-start
  768.7 24.8 %all-gather.13.cloned.1.call-done = bf16[512,1024]{0,1:T(8,128)(2,1)} async-done(((bf16[256,1024]{0,1:T(8,128)(2,1)}), bf16[512,1024]{0,1:T(8,128)(2,1)}) %all-gather.13.cloned.1.call-update) | async-done | bytes 1048592 | tf_op jit(solution)/shard_map/all_gather | solution.py:31
  793.5 0.0 copy-start.2
  793.5 1.8 convolution_bitcast_fusion.3
  795.3 0.0 copy-done.1
  795.3 2.5 fusion.9
  797.8 0.0 all-gather.15.cloned.1.call-update
  797.8 0.0 all-gather.17.cloned.1.call-start
  797.9 24.9 %all-gather.15.cloned.1.call-done = bf16[512,1024]{1,0:T(8,128)(2,1)} async-done(((bf16[256,1024]{1,0:T(8,128)(2,1)}), bf16[512,1024]{1,0:T(8,128)(2,1)}) %all-gather.15.cloned.1.call-update) | async-done | bytes 1048592 | tf_op jit(solution)/shard_map/all_gather | solution.py:26
  822.7 2.5 convolution_convert_fusion.1
  825.3 0.0 all-gather.17.cloned.1.call-update
  825.3 0.0 all-gather.19.cloned.1.call-start
  825.4 0.0 copy-done.2
  825.4 1.4 convolution_bitcast_fusion.1
  826.8 23.4 %all-gather.17.cloned.1.call-done = bf16[512,1024]{0,1:T(8,128)(2,1)} async-done(((bf16[256,1024]{0,1:T(8,128)(2,1)}), bf16[512,1024]{0,1:T(8,128)(2,1)}) %all-gather.17.cloned.1.call-update) | async-done | bytes 1048592 | tf_op jit(solution)/shard_map/all_gather | solution.py:31
  850.2 1.7 convolution_bitcast_fusion
  851.9 2.6 fusion.8
  854.5 0.0 all-gather.19.cloned.1.call-update
  854.5 24.9 %all-gather.19.cloned.1.call-done = bf16[512,1024]{1,0:T(8,128)(2,1)} async-done(((bf16[256,1024]{1,0:T(8,128)(2,1)}), bf16[512,1024]{1,0:T(8,128)(2,1)}) %all-gather.19.cloned.1.call-update) | async-done | bytes 1048592 | tf_op jit(solution)/shard_map/all_gather | solution.py:26
  879.5 1.7 fusion.11
  881.2 1.6 pad_maximum_fusion
  882.8 2.4 copy.6
Async XLA Ops:
  6.5 672.4 %all-reduce.2.cloned.1.call-start = ((), (), s32[]{:S(2)}) async-start(), calls=%async_computation | async-start | bytes 8388608 | tf_op jit(solution)/shard_map/psum | solution.py:9
  25.6 685.1 %all-gather.21.cloned.1.call-start = ((), (), s32[]{:S(2)}) async-start(), calls=%async_computation.7 | async-start | bytes 1572864 | tf_op jit(solution)/shard_map/all_gather | solution.py:26
  683.4 1.9 copy-start
  686.2 52.0 %all-gather.9.cloned.1.call-start = ((), (), s32[]{:S(2)}) async-start(), calls=%async_computation.1 | async-start | bytes 1572864 | tf_op jit(solution)/shard_map/all_gather | solution.py:31
  713.3 52.7 %all-gather.11.cloned.1.call-start = ((), (), s32[]{:S(2)}) async-start(), calls=%async_computation.2 | async-start | bytes 1572864 | tf_op jit(solution)/shard_map/all_gather | solution.py:26
  738.2 57.1 %copy-start.1 = (bf16[512,1024]{0,1:T(8,128)(2,1)S(1)}, bf16[512,1024]{0,1:T(8,128)(2,1)}, u32[]{:S(2)}) copy-start(bf16[512,1024]{0,1:T(8,128)(2,1)} %all-gather.9.cloned.1.call-done) | copy-start | bytes 3145732
  741.1 52.4 %all-gather.13.cloned.1.call-start = ((), (), s32[]{:S(2)}) async-start(), calls=%async_computation.3 | async-start | bytes 1572864 | tf_op jit(solution)/shard_map/all_gather | solution.py:31
  768.6 54.1 %all-gather.15.cloned.1.call-start = ((), (), s32[]{:S(2)}) async-start(), calls=%async_computation.4 | async-start | bytes 1572864 | tf_op jit(solution)/shard_map/all_gather | solution.py:26
  793.5 31.8 %copy-start.2 = (bf16[512,1024]{0,1:T(8,128)(2,1)S(1)}, bf16[512,1024]{0,1:T(8,128)(2,1)}, u32[]{:S(2)}) copy-start(bf16[512,1024]{0,1:T(8,128)(2,1)} %all-gather.13.cloned.1.call-done) | copy-start | bytes 3145732
  797.8 52.4 %all-gather.17.cloned.1.call-start = ((), (), s32[]{:S(2)}) async-start(), calls=%async_computation.5 | async-start | bytes 1572864 | tf_op jit(solution)/shard_map/all_gather | solution.py:31
  825.3 54.2 %all-gather.19.cloned.1.call-start = ((), (), s32[]{:S(2)}) async-start(), calls=%async_computation.6 | async-start | bytes 1572864 | tf_op jit(solution)/shard_map/all_gather | solution.py:26
Sparse Core Ops, SparseCore 0:
  25.7 653.1 all-reduce.1
  686.3 24.3 all-gather.20
  713.4 24.7 all-gather.8
  741.3 24.7 all-gather.10
  768.8 24.7 all-gather.12
  797.9 24.7 all-gather.14
  825.4 24.7 all-gather.16
  854.7 24.7 all-gather.18
where the time goes:
time: 892 us
  waiting for transfers between devices  823 us (92%)
  matrix products  41.4 us (5%)
  between operations  13.6 us (2%)
    psum x1, waiting for transfers between devices, shards(): totals = lax.psum(partial_value, 'blk')  653 us
    all_gather x4, waiting for transfers between devices, shards(): lax.all_gather(residual, 'rows', axis=0, tiled=True)  99.1 us
    all_gather x3, waiting for transfers between devices, shards(): full_blocks.append(lax.all_gather(solved_part, 'rows', axis=0, tiled=True))  69.9 us
    dot_general x1, matrix products, shards(): jnp.einsum('ksc,cr->ksr', panel, solved, preferred_element_type=jnp.float32)  19 us
  transfers between devices with their start and end apart: 8, of which 8 were waited for; matrix products, arithmetic and copies ran while one was open for 1% of the time, Pallas kernels for 0%

commit v1 on v0

--- a/solution.py
+++ b/solution.py
@@ -23,7 +23,9 @@
         inverse_now = inverses[current]
         solved_part = jnp.dot(
             inverse_now,
-            lax.all_gather(residual, "rows", axis=0, tiled=True),
+            jnp.concatenate(
+                lax.all_to_all(jnp.stack([residual] * lax.axis_size("rows")), "rows", 0, 0), axis=0
+            ),
             preferred_element_type=jnp.float32,
         ).astype(jnp.bfloat16)
         own_rows.append(solved_part)

time: 892 us -> 851 us (0.954)
  waiting for transfers between devices: 823 us -> 725 us
  blocking collectives: 0 us -> 61.3 us
    all_gather x4 -> x0, waiting for transfers between devices: 99.1 us -> none  [shards(): lax.all_gather(residual, 'rows', axis=0, tiled=True)]
    all_to_all x0 -> x4, blocking collectives: none -> 61.3 us  [shards(): lax.all_to_all(jnp.stack([residual] * lax.axis_size('rows')), 'rows', 0, 0)]
  transfers between devices with their start and end apart: 8 -> 4, of which waited for: 8 -> 4; matrix products, arithmetic and copies ran while one was open for 1% -> 1% of each run, Pallas kernels for 0% -> 0%
where the time goes in v1:
time: 851 us; the launch traced here: 850 us
  waiting for transfers between devices  725 us (85%)
  blocking collectives  61.3 us (7%)
  matrix products  37.7 us (4%)
  between operations  13.3 us (2%)
    psum x1, waiting for transfers between devices, shards(): totals = lax.psum(partial_value, 'blk')  653 us
    all_gather x3, waiting for transfers between devices, shards(): full_blocks.append(lax.all_gather(solved_part, 'rows', axis=0, tiled=True))  71.7 us
    all_to_all x4, blocking collectives, shards(): lax.all_to_all(jnp.stack([residual] * lax.axis_size('rows')), 'rows', 0, 0)  61.3 us
    dot_general x1, matrix products, shards(): jnp.einsum('ksc,cr->ksr', panel, solved, preferred_element_type=jnp.float32)  19 us
  transfers between devices with their start and end apart: 4, of which 4 were waited for; matrix products, arithmetic and copies ran while one was open for 1% of the time, Pallas kernels for 0%

profile of v1, /device:TPU:1, one launch (start us, length us, event | category | flops | bytes accessed | tf_op | source)
XLA Modules:
  0.0 850.0 jit_solution(10565429064364186751)
XLA Ops:
  6.5 0.0 all-reduce.2.cloned.1.call-start
  6.5 19.0 %fusion = f32[4,256,1024]{2,1,0:T(8,128)} fusion(bf16[4,256,6144]{2,1,0:T(8,128)(2,1)} %param.5, bf16[6144,1024]{1,0:T(8,128)(2,1)} %param.6), kind=kOutput, calls=%fused_computation | convolution fusion | flops 12884901888 | bytes 29360128 | tf_op jit(solution)/shard_map/ksc,cr->ksr/dot_general | solution.py:8
  25.6 0.0 all-reduce.2.cloned.1.call-update
  25.6 0.0 all-gather.4.cloned.1.call-start
  25.6 653.3 %all-reduce.2.cloned.1.call-done = f32[4,256,1024]{2,1,0:T(8,128)} async-done(((f32[4,256,1024]{2,1,0:T(8,128)}), f32[4,256,1024]{2,1,0:T(8,128)}) %all-reduce.2.cloned.1.call-update) | async-done | bytes 4194320 | tf_op jit(solution)/shard_map/psum | solution.py:9
  678.9 4.4 sub.21
  683.3 0.0 copy-start
  683.4 2.0 copy-done
  685.3 0.1 slice.123
  685.4 0.1 pad_maximum_fusion.1
  685.5 15.2 %all_to_all.20 = bf16[2,256,1024]{2,1,0:T(8,128)(2,1)S(1)} all-to-all(bf16[2,256,1024]{2,1,0:T(8,128)(2,1)S(1)} %pad_maximum_fusion.1), channel_id=1, replica_groups=mesh['blk'=64,'rows'=2] {'rows'}, dimensions={0} | all-to-all | bytes 2097152 | tf_op jit(solution)/shard_map/all_to_all | solution.py:27
  700.7 2.2 convolution_convert_fusion.3
  703.0 0.0 all-gather.4.cloned.1.call-update
  703.0 0.0 all-gather.6.cloned.1.call-start
  703.0 3.1 slice_bitcast_fusion.3
  706.1 21.7 %all-gather.4.cloned.1.call-done = bf16[512,1024]{0,1:T(8,128)(2,1)} async-done(((bf16[256,1024]{0,1:T(8,128)(2,1)}), bf16[512,1024]{0,1:T(8,128)(2,1)}) %all-gather.4.cloned.1.call-update) | async-done | bytes 1048592 | tf_op jit(solution)/shard_map/all_gather | solution.py:33
  727.8 2.0 fusion.11
  729.8 0.0 copy-start.1
  729.8 0.1 pad_maximum_fusion.2
  729.9 15.4 %all_to_all.21 = bf16[2,256,1024]{2,1,0:T(8,128)(2,1)S(1)} all-to-all(bf16[2,256,1024]{2,1,0:T(8,128)(2,1)S(1)} %pad_maximum_fusion.2), channel_id=1, replica_groups=mesh['blk'=64,'rows'=2] {'rows'}, dimensions={0} | all-to-all | bytes 2097152 | tf_op jit(solution)/shard_map/all_to_all | solution.py:27
  745.4 2.2 convolution_convert_fusion.2
  747.6 0.0 all-gather.6.cloned.1.call-update
  747.6 0.0 all-gather.8.cloned.1.call-start
  747.7 25.7 %all-gather.6.cloned.1.call-done = bf16[512,1024]{0,1:T(8,128)(2,1)} async-done(((bf16[256,1024]{0,1:T(8,128)(2,1)}), bf16[512,1024]{0,1:T(8,128)(2,1)}) %all-gather.6.cloned.1.call-update) | async-done | bytes 1048592 | tf_op jit(solution)/shard_map/all_gather | solution.py:33
  773.4 1.7 convolution_bitcast_fusion.3
  775.1 0.0 copy-done.1
  775.1 0.0 copy-start.2
  775.1 1.8 fusion.12
  776.9 0.1 pad_maximum_fusion.3
  777.0 15.3 %all_to_all.22 = bf16[2,256,1024]{2,1,0:T(8,128)(2,1)S(1)} all-to-all(bf16[2,256,1024]{2,1,0:T(8,128)(2,1)S(1)} %pad_maximum_fusion.3), channel_id=1, replica_groups=mesh['blk'=64,'rows'=2] {'rows'}, dimensions={0} | all-to-all | bytes 2097152 | tf_op jit(solution)/shard_map/all_to_all | solution.py:27
  792.3 2.2 convolution_convert_fusion.1
  794.5 0.0 all-gather.8.cloned.1.call-update
  794.5 0.0 copy-done.2
  794.5 1.4 convolution_bitcast_fusion.1
  796.0 24.3 %all-gather.8.cloned.1.call-done = bf16[512,1024]{0,1:T(8,128)(2,1)} async-done(((bf16[256,1024]{0,1:T(8,128)(2,1)}), bf16[512,1024]{0,1:T(8,128)(2,1)}) %all-gather.8.cloned.1.call-update) | async-done | bytes 1048592 | tf_op jit(solution)/shard_map/all_gather | solution.py:33
  820.3 1.7 convolution_bitcast_fusion
  822.0 0.0 copy-start.3
  822.0 0.0 copy-start.4
  822.0 0.0 copy-start.5
  822.0 1.9 fusion.13
  823.9 0.1 pad_maximum_fusion.4
  824.0 15.3 %all_to_all.23 = bf16[2,256,1024]{2,1,0:T(8,128)(2,1)S(1)} all-to-all(bf16[2,256,1024]{2,1,0:T(8,128)(2,1)S(1)} %pad_maximum_fusion.4), channel_id=1, replica_groups=mesh['blk'=64,'rows'=2] {'rows'}, dimensions={0} | all-to-all | bytes 2097152 | tf_op jit(solution)/shard_map/all_to_all | solution.py:27
  839.3 1.4 fusion.14
  840.8 0.0 copy-done.3
  840.8 0.0 copy-done.4
  840.8 0.0 copy-done.5
  840.8 0.3 pad_maximum_fusion
  841.1 2.4 copy.12
Async XLA Ops:
  6.5 672.4 %all-reduce.2.cloned.1.call-start = ((), (), s32[]{:S(2)}) async-start(), calls=%async_computation.4 | async-start | bytes 8388608 | tf_op jit(solution)/shard_map/psum | solution.py:9
  25.6 702.2 %all-gather.4.cloned.1.call-start = ((), (), s32[]{:S(2)}) async-start(), calls=%async_computation.5 | async-start | bytes 1572864 | tf_op jit(solution)/shard_map/all_gather | solution.py:33
  683.3 2.0 copy-start
  703.0 70.4 %all-gather.6.cloned.1.call-start = ((), (), s32[]{:S(2)}) async-start(), calls=%async_computation.6 | async-start | bytes 1572864 | tf_op jit(solution)/shard_map/all_gather | solution.py:33
  729.8 45.2 %copy-start.1 = (bf16[512,1024]{0,1:T(8,128)(2,1)S(1)}, bf16[512,1024]{0,1:T(8,128)(2,1)}, u32[]{:S(2)}) copy-start(bf16[512,1024]{0,1:T(8,128)(2,1)} %all-gather.4.cloned.1.call-done) | copy-start | bytes 3145732
  747.6 72.7 %all-gather.8.cloned.1.call-start = ((), (), s32[]{:S(2)}) async-start(), calls=%async_computation.7 | async-start | bytes 1572864 | tf_op jit(solution)/shard_map/all_gather | solution.py:33
  775.1 19.5 %copy-start.2 = (bf16[512,1024]{0,1:T(8,128)(2,1)S(1)}, bf16[512,1024]{0,1:T(8,128)(2,1)}, u32[]{:S(2)}) copy-start(bf16[512,1024]{0,1:T(8,128)(2,1)} %all-gather.6.cloned.1.call-done) | copy-start | bytes 3145732
  822.0 18.8 %copy-start.3 = (bf16[1024,256]{1,0:T(8,128)(2,1)S(1)}, bf16[1024,256]{1,0:T(8,128)(2,1)}, u32[]{:S(2)}) copy-start(bf16[1024,256]{1,0:T(8,128)(2,1)} %convolution_convert_fusion.3) | copy-start | bytes 1572868
  822.0 18.8 %copy-start.4 = (bf16[1024,256]{1,0:T(8,128)(2,1)S(1)}, bf16[1024,256]{1,0:T(8,128)(2,1)}, u32[]{:S(2)}) copy-start(bf16[1024,256]{1,0:T(8,128)(2,1)} %convolution_convert_fusion.2) | copy-start | bytes 1572868
  822.0 18.8 %copy-start.5 = (bf16[1024,256]{1,0:T(8,128)(2,1)S(1)}, bf16[1024,256]{1,0:T(8,128)(2,1)}, u32[]{:S(2)}) copy-start(bf16[1024,256]{1,0:T(8,128)(2,1)} %convolution_convert_fusion.1) | copy-start | bytes 1572868
Sparse Core Ops, SparseCore 0:
  25.7 653.1 all-reduce.1
  703.1 24.6 all-gather.3
  747.7 25.5 all-gather.5
  794.7 25.5 all-gather.7
